TPU v7x, 32 devices: a whole 2x2x4 slice. The times are simulated.
32 devices in a mesh: gx: 4 (over z), gy: 4 (over x, core), gz: 2 (over y).
Axes of the slice: x: 2, y: 2, z: 4, core: 2. Of those that a mesh axis runs over, the one named last changes fastest.
Arguments:
- elevation: float32 [256, 8192], P('gx', ('gy', 'gz')), may hold values from -1 to 1
- surface_potential: float32 [256, 8192], P('gx', ('gy', 'gz')), may hold values from -2 to 2
- seabed: int32 [256, 8192], P('gx', 'gy'), may hold values from 384 to 1023
- interior_potential: float32 [16, 256, 8192], P('gz', 'gx', 'gy'), may hold values from -1.5 to 1.5
Outputs:
- new_elevation: float32 [256, 8192], P('gx', ('gy', 'gz'))
- new_potential: float32 [256, 8192], P('gx', ('gy', 'gz'))
- laplace_apply: float32 [16, 256, 8192], P('gz', 'gx', 'gy')
All inputs are finite; a program needn't handle non-finite values.
Results may differ from a plain program's by a relative error of at most 0.0003.
Values sent between devices are 32-bit elements; how exact they have to be, the bound alone decides.
No kernel may reach another device: no remote copies, remote signals or barrier semaphores. Data moves between devices by JAX's collectives and lax.ppermute only.
A program may use at most 64 MiB of HBM per device.

v0:
```python
import jax
import jax.numpy as jnp
from jax import lax
from jax.sharding import PartitionSpec as P

time_step = 0.05
depth_unit = 0.015625


def with_halo(block, sides, width):
    for axis, dim in sides:
        count = lax.axis_size(axis)
        forward = [(i, i + 1) for i in range(count - 1)]
        forward.append((count - 1, 0))
        backward = [(target, source) for source, target in forward]
        low = lax.ppermute(
            lax.slice_in_dim(block, block.shape[dim] - width, None, axis=dim), axis, forward
        )
        high = lax.ppermute(lax.slice_in_dim(block, 0, width, axis=dim), axis, backward)
        block = jnp.concatenate([low, block, high], axis=dim)
    return block


def partner_2(value, axis, bit):
    mask = 2**bit
    pairs = [(source, source ^ mask) for source in range(lax.axis_size(axis))]
    return lax.ppermute(value, axis, pairs)


def window(extended, step_north, step_east, margin):
    height = extended.shape[-2] - 2 * margin
    breadth = extended.shape[-1] - 2 * margin
    return extended[
        ...,
        margin + step_north : margin + step_north + height,
        margin + step_east : margin + step_east + breadth,
    ]


def rates(extended):
    grad_north = (
        8.0 * (window(extended, 1, 0, 2) - window(extended, -1, 0, 2))
        - (window(extended, 2, 0, 2) - window(extended, -2, 0, 2))
    ) / 12.0
    grad_east = (
        8.0 * (window(extended, 0, 1, 2) - window(extended, 0, -1, 2))
        - (window(extended, 0, 2, 2) - window(extended, 0, -2, 2))
    ) / 12.0
    centre = window(extended, 0, 0, 2)
    poten = extended[1]
    curve_north = (
        -window(poten, 2, 0, 2)
        + 16.0 * window(poten, 1, 0, 2)
        - 30.0 * centre[1]
        + 16.0 * window(poten, -1, 0, 2)
        - window(poten, -2, 0, 2)
    )
    curve_east = (
        -window(poten, 0, 2, 2)
        + 16.0 * window(poten, 0, 1, 2)
        - 30.0 * centre[1]
        + 16.0 * window(poten, 0, -1, 2)
        - window(poten, 0, -2, 2)
    )
    curvature = (curve_north + curve_east) / 12.0
    rate_height = curvature - (grad_north[0] * grad_north[1] + grad_east[0] * grad_east[1])
    rate_potential = -centre[0] - 0.5 * (
        grad_north[1] * grad_north[1] + grad_east[1] * grad_east[1]
    )
    return jnp.stack([rate_height, rate_potential])


def shards(elevation, surface_potential, seabed, interior_potential):
    surface_pair = jnp.stack([elevation, surface_potential])
    depth = seabed.astype(jnp.float32) * depth_unit
    layers = interior_potential.shape[0]
    surface_tile = lax.all_gather(surface_pair, "gz", axis=2, tiled=True)
    triple = jnp.concatenate([surface_tile, depth[None]], 0)
    deep_wide = with_halo(triple, (("gx", 1), ("gy", 2)), 5)
    start_pair = deep_wide[:2]
    section_one = start_pair[:, 2:-2, 2:-2] + time_step * rates(start_pair)
    surface_rim = 0.5 * (
        start_pair[:, 4:-4, 4:-4] + section_one[:, 2:-2, 2:-2] + time_step * rates(section_one)
    )
    depth_rim = deep_wide[2, 4:-4, 4:-4]
    plane_wide = jnp.stack([depth_rim + surface_rim[0], surface_rim[1], depth_rim])
    own_width = surface_pair.shape[2]
    updated = lax.dynamic_slice_in_dim(
        surface_rim[:, 1:-1, 1:-1], lax.axis_index("gz") * own_width, own_width, 2
    )
    volume_wide = with_halo(interior_potential, (("gx", 1), ("gy", 2)), 1)
    layer_group = lax.axis_index("gz")
    bottom_group = layer_group == 0
    outgoing = jnp.where(bottom_group, volume_wide[-1], volume_wide[0])
    partner = partner_2(outgoing, "gz", 0)
    ghost_below = jnp.where(bottom_group, volume_wide[0], partner)
    ghost_above = jnp.where(bottom_group, partner, 2.0 * plane_wide[1] - volume_wide[-1])
    column_stack = jnp.concatenate([ghost_below[None], volume_wide, ghost_above[None]], 0)
    column_centre = plane_wide[0, 1:-1, 1:-1]
    column_north = 0.5 * (plane_wide[0, 2:, 1:-1] - plane_wide[0, :-2, 1:-1])
    column_east = 0.5 * (plane_wide[0, 1:-1, 2:] - plane_wide[0, 1:-1, :-2])
    depth_north = 0.5 * (plane_wide[2, 2:, 1:-1] - plane_wide[2, :-2, 1:-1])
    depth_east = 0.5 * (plane_wide[2, 1:-1, 2:] - plane_wide[2, 1:-1, :-2])
    total_layers = layers * lax.axis_size("gz")
    sigma_level = (
        (layer_group * layers + jnp.arange(layers, dtype=jnp.int32)).astype(jnp.float32) + 0.5
    ) / total_layers
    sigma_level = sigma_level[:, None, None]
    slope_north = (depth_north - sigma_level * column_north) / column_centre
    slope_east = (depth_east - sigma_level * column_east) / column_centre
    spacing = 1.0 / total_layers
    middle_stack = column_stack[1:-1]
    upper_stack = column_stack[2:]
    lower_stack = column_stack[:-2]
    centre = middle_stack[:, 1:-1, 1:-1]
    second_north = middle_stack[:, 2:, 1:-1] - 2.0 * centre + middle_stack[:, :-2, 1:-1]
    second_east = middle_stack[:, 1:-1, 2:] - 2.0 * centre + middle_stack[:, 1:-1, :-2]
    mixed_north = (
        upper_stack[:, 2:, 1:-1]
        - upper_stack[:, :-2, 1:-1]
        - lower_stack[:, 2:, 1:-1]
        + lower_stack[:, :-2, 1:-1]
    ) / (4.0 * spacing)
    mixed_east = (
        upper_stack[:, 1:-1, 2:]
        - upper_stack[:, 1:-1, :-2]
        - lower_stack[:, 1:-1, 2:]
        + lower_stack[:, 1:-1, :-2]
    ) / (4.0 * spacing)
    vertical = (upper_stack[:, 1:-1, 1:-1] - 2.0 * centre + lower_stack[:, 1:-1, 1:-1]) / (
        spacing * spacing
    )
    weight = (
        slope_north * slope_north + slope_east * slope_east + 1.0 / (column_centre * column_centre)
    )
    laplace_apply = (
        second_north
        + second_east
        + 2.0 * slope_north * mixed_north
        + 2.0 * slope_east * mixed_east
        + weight * vertical
    )
    return (updated[0], updated[1], laplace_apply)


def solution(mesh):
    return jax.shard_map(
        shards,
        mesh=mesh,
        in_specs=(P("gx", ("gy", "gz")), P("gx", ("gy", "gz")), P("gx", "gy"), P("gz", "gx", "gy")),
        out_specs=(P("gx", ("gy", "gz")), P("gx", ("gy", "gz")), P("gz", "gx", "gy")),
        check_vma=False,
    )
```

profile of v0, /device:TPU:1, one launch (start us, length us, event | category | flops | bytes accessed | tf_op | source)
XLA Modules:
  0.0 121.5 jit_solution(9207310284389499734)
XLA Ops:
  7.2 0.0 all-gather.2.cloned.1.call-start
  7.2 1.9 %pad_maximum_fusion.24 = f32[2,64,1024]{2,1,0:T(8,128)} fusion(f32[1,64,1024]{2,1,0:T(8,128)} %bitcast.74, f32[1,64,1024]{2,1,0:T(8,128)} %bitcast.75), kind=kLoop, calls=%fused_computation.172 | loop fusion | flops 131072 | bytes 1048576 | tf_op jit(solution)/shard_map/stack | solution.py:74
  9.1 0.0 all-gather.2.cloned.1.call-update
  9.1 1.3 %fusion.87 = (f32[8,1,2048]{2,1,0:T(1,128)S(1)}, f32[8,1,2048]{2,1,0:T(1,128)S(1)}) fusion(f32[8,64,2048]{2,1,0:T(8,128)} %param.7), kind=kLoop, calls=%fused_computation.182 | loop fusion | bytes 262144 | tf_op jit(solution)/shard_map/slice | solution.py:17
  10.4 2.2 %collective-permute-start.5 = (f32[8,1,2048]{2,1,0:T(1,128)S(1)}, f32[8,1,2048]{2,1,0:T(1,128)S(1)}, u32[]{:S(2)}, u32[]{:S(2)}) collective-permute-start(f32[8,1,2048]{2,1,0:T(1,128)S(1)} %get-tuple-element.7), channel_id=1, source_target_pairs={{0,8},{8,16},{16,24},{24,0},{1,9},{9,17},{17,25},{25,1},{2,10},{10... | collective-permute-start | bytes 196616 | tf_op jit(solution)/shard_map/ppermute | solution.py:16
  12.6 2.1 %collective-permute-start.4 = (f32[8,1,2048]{2,1,0:T(1,128)S(1)}, f32[8,1,2048]{2,1,0:T(1,128)S(1)}, u32[]{:S(2)}, u32[]{:S(2)}) collective-permute-start(f32[8,1,2048]{2,1,0:T(1,128)S(1)} %get-tuple-element.8), channel_id=1, source_target_pairs={{8,0},{16,8},{24,16},{0,24},{9,1},{17,9},{25,17},{1,25},{10,2},{18... | collective-permute-start | bytes 196616 | tf_op jit(solution)/shard_map/ppermute | solution.py:19
  14.7 1.1 multiply_bitcast_fusion
  15.8 0.6 collective-permute-done.5
  16.4 0.3 collective-permute-done.4
  16.7 5.5 %pad_maximum_fusion = f32[8,66,2048]{2,1,0:T(8,128)} fusion(f32[8,1,2048]{2,1,0:T(1,128)S(1)} %collective-permute-done.4, f32[8,64,2048]{2,1,0:T(8,128)} %param.7, f32[8,1,2048]{2,1,0:T(1,128)S(1)} %collective-permute-done.5), kind=kLoop, calls=%fused_computation.16 | loop fusion | flops 2162688 | bytes 8650752 | tf_op jit(solution)/shard_map/concatenate | solution.py:20
  22.2 11.1 %all-gather.2.cloned.1.call-done = f32[2,64,2048]{2,1,0:T(8,128)} async-done(((f32[2,64,1024]{2,1,0:T(8,128)}), f32[2,64,2048]{2,1,0:T(8,128)}) %all-gather.2.cloned.1.call-update) | async-done | bytes 1048592 | tf_op jit(solution)/shard_map/all_gather | solution.py:77
  33.3 1.7 %pad_maximum_fusion.26 = (f32[3,5,2048]{2,1,0:T(8,128)}, f32[3,5,2048]{2,1,0:T(8,128)S(1)}) fusion(f32[1,64,2048]{2,1,0:T(8,128)S(1)} %multiply_bitcast_fusion, f32[2,64,2048]{2,1,0:T(8,128)} %all-gather.2.cloned.1.call-done), kind=kLoop, calls=%fused_computation.179 | loop fusion | flops 61440 | bytes 1818624 | tf_op jit(solution)/shard_map/slice | solution.py:17
  35.0 1.2 collective-permute-start
  36.2 2.1 %collective-permute-start.1 = (f32[3,5,2048]{2,1,0:T(8,128)S(1)}, f32[3,5,2048]{2,1,0:T(8,128)S(1)}, u32[]{:S(2)}, u32[]{:S(2)}) collective-permute-start(f32[3,5,2048]{2,1,0:T(8,128)S(1)} %get-tuple-element.16), channel_id=1, source_target_pairs={{8,0},{16,8},{24,16},{0,24},{9,1},{17,9},{25,17},{1,25},{10,2},{18... | collective-permute-start | bytes 368648 | tf_op jit(solution)/shard_map/ppermute | solution.py:19
  38.2 1.2 fusion.86
  39.4 1.5 %collective-permute-start.6 = (f32[8,66,1]{2,1,0:T(8,128)S(1)}, f32[8,66,1]{2,1,0:T(8,128)S(1)}, u32[]{:S(2)}, u32[]{:S(2)}) collective-permute-start(f32[8,66,1]{2,1,0:T(8,128)S(1)} %get-tuple-element.5), channel_id=1, source_target_pairs={{2,0},{4,2},{6,4},{0,6},{3,1},{5,3},{7,5},{1,7},{10,8},{12,10},{14... | collective-permute-start | bytes 6344 | tf_op jit(solution)/shard_map/ppermute | solution.py:19
  40.9 1.1 collective-permute-start.7
  42.0 0.5 add_multiply_fusion
  42.6 7.1 %collective-permute-done.6 = f32[8,66,1]{2,1,0:T(8,128)S(1)} collective-permute-done((f32[8,66,1]{2,1,0:T(8,128)S(1)}, f32[8,66,1]{2,1,0:T(8,128)S(1)}, u32[]{:S(2)}, u32[]{:S(2)}) %collective-permute-start.6) | collective-permute-done | bytes 2144 | tf_op jit(solution)/shard_map/ppermute | solution.py:19
  49.7 7.0 %concatenate.56 = f32[8,66,2050]{2,1,0:T(8,128)} concatenate(f32[8,66,1]{2,1,0:T(8,128)S(1)} %collective-permute-done.7, f32[8,66,2048]{2,1,0:T(8,128)} %pad_maximum_fusion, f32[8,66,1]{2,1,0:T(8,128)S(1)} %collective-permute-done.6), dimensions={2} | concatenate | bytes 8659200 | tf_op jit(solution)/shard_map/concatenate | solution.py:20
  56.6 0.0 collective-permute-done
  56.7 0.3 pad_maximum_fusion.11
  57.0 0.0 copy-start.2
  57.0 0.1 fusion.88
  57.1 0.5 collective-permute-start.3
  57.6 1.3 %collective-permute-start.2 = (f32[3,74,5]{2,1,0:T(8,128)S(1)}, f32[3,74,5]{2,1,0:T(8,128)}, u32[]{:S(2)}, u32[]{:S(2)}) collective-permute-start(f32[3,74,5]{2,1,0:T(8,128)S(1)} %get-tuple-element.14), channel_id=1, source_target_pairs={{0,2},{2,4},{4,6},{6,0},{1,3},{3,5},{5,7},{7,1},{8,10},{10,12},{12... | collective-permute-start | bytes 13328 | tf_op jit(solution)/shard_map/ppermute | solution.py:16
  58.9 2.2 %fusion.75 = f32[66,2050]{1,0:T(8,128)} fusion(f32[8,66,2050]{2,1,0:T(8,128)} %concatenate.56, pred[]{:T(512)S(6)} %eq.3), kind=kLoop, calls=%fused_computation.147 | loop fusion | flops 135300 | bytes 1623601 | tf_op jit(solution)/shard_map/jit(_where)/select_n | solution.py:94
  61.1 0.3 collective-permute-start.8
  61.3 1.8 %collective-permute-done.3 = f32[3,74,5]{2,1,0:T(8,128)S(1)} collective-permute-done((f32[3,74,5]{2,1,0:T(8,128)S(1)}, f32[3,74,5]{2,1,0:T(8,128)S(1)}, u32[]{:S(2)}, u32[]{:S(2)}) %collective-permute-start.3) | collective-permute-done | bytes 4472 | tf_op jit(solution)/shard_map/ppermute | solution.py:19
  63.2 0.6 copy-done.7
  63.8 0.0 collective-permute-done.2
  63.8 3.0 %concatenate.48 = f32[3,74,2058]{2,1,0:T(8,128)S(1)} concatenate(f32[3,74,5]{2,1,0:T(8,128)} %collective-permute-done.2, f32[3,74,2048]{2,1,0:T(8,128)} %copy-done.2, f32[3,74,5]{2,1,0:T(8,128)} %copy-done.7), dimensions={2} | concatenate | bytes 3655008 | tf_op jit(solution)/shard_map/concatenate | solution.py:20
  66.9 2.4 %fusion.41 = (f32[2,70,2054]{2,1,0:T(8,128)S(1)}, f32[2,70,2054]{2,1,0:T(8,128)S(1)}) fusion(f32[3,74,2058]{2,1,0:T(8,128)S(1)} %concatenate.48), kind=kLoop, calls=%fused_computation.78 | loop fusion | flops 2875600 | bytes 11502400 | tf_op jit(solution)/shard_map/div | solution.py:41
  69.3 0.3 fusion.61
  69.6 1.4 %fusion.65 = f32[1,70,2054]{2,1,0:T(8,128)S(1)} fusion(f32[2,70,2054]{2,1,0:T(8,128)S(1)} %get-tuple-element.10, f32[2,70,2054]{2,1,0:T(8,128)S(1)} %get-tuple-element.9, f32[74,2058]{1,0:T(8,128)S(1)} %slice_bitcast_fusion, f32[3,74,2058]{2,1,0:T(8,128)S(1)} %concatenate.48), kind=kLoop, calls=%fused_computation.126 | loop fusion | flops 3019380 | bytes 8051680 | tf_op jit(solution)/shard_map/stack | solution.py:70
  71.0 0.4 slice_add_fusion.1
  71.4 2.4 %fusion.33 = (f32[2,66,2050]{2,1,0:T(8,128)S(1)}, f32[2,66,2050]{2,1,0:T(8,128)S(1)}) fusion(f32[2,70,2054]{2,1,0:T(8,128)S(1)} %slice_add_fusion.1), kind=kLoop, calls=%fused_computation.65 | loop fusion | flops 2706000 | bytes 10824000 | tf_op jit(solution)/shard_map/div | solution.py:41
  73.9 0.3 fusion.47
  74.2 1.4 %fusion.51 = f32[1,66,2050]{2,1,0:T(8,128)S(1)} fusion(f32[2,66,2050]{2,1,0:T(8,128)S(1)} %get-tuple-element.18, f32[2,66,2050]{2,1,0:T(8,128)S(1)} %get-tuple-element.17, f32[70,2054]{1,0:T(8,128)S(1)} %slice_bitcast_fusion.3, f32[2,70,2054]{2,1,0:T(8,128)S(1)} %slice_add_fusion.1), kind=kLoop, calls=%fused_computation.99 | loop fusion | flops 2841300 | bytes 7576800 | tf_op jit(solution)/shard_map/stack | solution.py:70
  75.6 0.0 copy-start.8
  75.6 0.7 fusion.36
  76.3 0.2 slice_add_fusion.2
  76.6 0.3 slice.461
  77.0 2.5 %fusion.85 = (f32[64,2048]{1,0:T(8,128)}, f32[64,2048]{1,0:T(8,128)}) fusion(f32[3,5,2048]{2,1,0:T(8,128)S(1)} %collective-permute-done, f32[1,64,2048]{2,1,0:T(8,128)S(1)} %copy-done.4, f32[2,64,2048]{2,1,0:T(8,128)S(1)} %copy-done.1, f32[3,5,2048]{2,1,0:T(8,128)S(1)} %collective-permute-done.1, f32[3,74,5]{2,1,0:T(8,128)} %collective-permute-done.2, ...), kind=kLoop, calls=%fused_computation.168 | loop fusion | flops 2097152 | bytes 2876080 | tf_op jit(solution)/shard_map/sub | solution.py:109
  79.4 0.8 dynamic-slice_bitcast_fusion
  80.2 2.0 %fusion.82 = (f32[64,2048]{1,0:T(8,128)}, f32[64,2048]{1,0:T(8,128)}, f32[64,2048]{1,0:T(8,128)}, f32[64,2048]{1,0:T(8,128)}) fusion(f32[1,66,2050]{2,1,0:T(8,128)S(1)} %slice_add_fusion.2), kind=kLoop, calls=%fused_computation.164 | loop fusion | flops 786432 | bytes 4718592 | tf_op jit(solution)/shard_map/mul | solution.py:109
  82.2 2.1 %fusion.46 = (f32[1,66,2050]{2,1,0:T(8,128)S(1)}, f32[1,66,2050]{2,1,0:T(8,128)}) fusion(f32[66,2050]{1,0:T(8,128)} %collective-permute-done.8, f32[2,66,2050]{2,1,0:T(8,128)S(1)} %fusion.36, f32[8,66,2050]{2,1,0:T(8,128)S(1)} %bitcast.73, pred[]{:T(512)S(6)} %eq.3), kind=kLoop, calls=%fused_computation.89 | loop fusion | flops 541200 | bytes 3247201 | tf_op jit(solution)/shard_map/broadcast_in_dim | solution.py:98
  84.3 30.3 %fusion.5 = f32[8,64,2048]{2,1,0:T(8,128)} fusion(f32[8,66,2050]{2,1,0:T(8,128)S(1)} %bitcast.73, f32[1,66,2050]{2,1,0:T(8,128)} %get-tuple-element.4, f32[1,66,2050]{2,1,0:T(8,128)S(1)} %get-tuple-element.3, f32[8,66,1]{2,1,0:T(8,128)} %copy-done.6, f32[8,1,2048]{2,1,0:T(1,128)} %copy-done.11, f32[8,64,2048]{2,1,0:T(8,128)S(1)} %copy-done, ...), kind=kLoop, calls=%fused_computation.22 | loop fusion | flops 55574528 | bytes 17081664 | tf_op jit(solution)/shard_map/add | solution.py:137
  (31 shorter events, 0.1 us)
Async XLA Ops:
  7.2 26.1 %all-gather.2.cloned.1.call-start = ((), (), s32[]{:S(2)}) async-start(), calls=%async_computation | async-start | bytes 1572864 | tf_op jit(solution)/shard_map/all_gather | solution.py:77
  10.4 5.9 %collective-permute-start.5 = (f32[8,1,2048]{2,1,0:T(1,128)S(1)}, f32[8,1,2048]{2,1,0:T(1,128)S(1)}, u32[]{:S(2)}, u32[]{:S(2)}) collective-permute-start(f32[8,1,2048]{2,1,0:T(1,128)S(1)} %get-tuple-element.7), channel_id=1, source_target_pairs={{0,8},{8,16},{16,24},{24,0},{1,9},{9,17},{17,25},{25,1},{2,10},{10... | collective-permute-start | bytes 196616 | tf_op jit(solution)/shard_map/ppermute | solution.py:16
  12.6 4.1 %collective-permute-start.4 = (f32[8,1,2048]{2,1,0:T(1,128)S(1)}, f32[8,1,2048]{2,1,0:T(1,128)S(1)}, u32[]{:S(2)}, u32[]{:S(2)}) collective-permute-start(f32[8,1,2048]{2,1,0:T(1,128)S(1)} %get-tuple-element.8), channel_id=1, source_target_pairs={{8,0},{16,8},{24,16},{0,24},{9,1},{17,9},{25,17},{1,25},{10,2},{18... | collective-permute-start | bytes 196616 | tf_op jit(solution)/shard_map/ppermute | solution.py:19
  15.8 40.9 %copy-start.3 = (f32[1,64,2048]{2,1,0:T(8,128)}, f32[1,64,2048]{2,1,0:T(8,128)S(1)}, u32[]{:S(2)}) copy-start(f32[1,64,2048]{2,1,0:T(8,128)S(1)} %multiply_bitcast_fusion) | copy-start | bytes 1572868
  16.4 5.8 %copy-start.9 = (f32[8,1,2048]{2,1,0:T(1,128)}, f32[8,1,2048]{2,1,0:T(1,128)S(1)}, u32[]{:S(2)}) copy-start(f32[8,1,2048]{2,1,0:T(1,128)S(1)} %collective-permute-done.5) | copy-start | bytes 196612
  16.7 5.5 %copy-start.11 = (f32[8,1,2048]{2,1,0:T(1,128)}, f32[8,1,2048]{2,1,0:T(1,128)S(1)}, u32[]{:S(2)}) copy-start(f32[8,1,2048]{2,1,0:T(1,128)S(1)} %collective-permute-done.4) | copy-start | bytes 196612
  35.0 21.7 %collective-permute-start = (f32[3,5,2048]{2,1,0:T(8,128)}, f32[3,5,2048]{2,1,0:T(8,128)S(1)}, u32[]{:S(2)}, u32[]{:S(2)}) collective-permute-start(f32[3,5,2048]{2,1,0:T(8,128)} %get-tuple-element.15), channel_id=1, source_target_pairs={{0,8},{8,16},{16,24},{24,0},{1,9},{9,17},{17,25},{25,1},{2,10},{10... | collective-permute-start | bytes 368648 | tf_op jit(solution)/shard_map/ppermute | solution.py:16
  36.2 20.5 %collective-permute-start.1 = (f32[3,5,2048]{2,1,0:T(8,128)S(1)}, f32[3,5,2048]{2,1,0:T(8,128)S(1)}, u32[]{:S(2)}, u32[]{:S(2)}) collective-permute-start(f32[3,5,2048]{2,1,0:T(8,128)S(1)} %get-tuple-element.16), channel_id=1, source_target_pairs={{8,0},{16,8},{24,16},{0,24},{9,1},{17,9},{25,17},{1,25},{10,2},{18... | collective-permute-start | bytes 368648 | tf_op jit(solution)/shard_map/ppermute | solution.py:19
  39.4 10.2 %collective-permute-start.6 = (f32[8,66,1]{2,1,0:T(8,128)S(1)}, f32[8,66,1]{2,1,0:T(8,128)S(1)}, u32[]{:S(2)}, u32[]{:S(2)}) collective-permute-start(f32[8,66,1]{2,1,0:T(8,128)S(1)} %get-tuple-element.5), channel_id=1, source_target_pairs={{2,0},{4,2},{6,4},{0,6},{3,1},{5,3},{7,5},{1,7},{10,8},{12,10},{14... | collective-permute-start | bytes 6344 | tf_op jit(solution)/shard_map/ppermute | solution.py:19
  40.9 8.8 %collective-permute-start.7 = (f32[8,66,1]{2,1,0:T(8,128)S(1)}, f32[8,66,1]{2,1,0:T(8,128)S(1)}, u32[]{:S(2)}, u32[]{:S(2)}) collective-permute-start(f32[8,66,1]{2,1,0:T(8,128)S(1)} %get-tuple-element.6), channel_id=1, source_target_pairs={{0,2},{2,4},{4,6},{6,0},{1,3},{3,5},{5,7},{7,1},{8,10},{10,12},{12... | collective-permute-start | bytes 6344 | tf_op jit(solution)/shard_map/ppermute | solution.py:16
  42.6 14.1 %copy-start.1 = (f32[2,64,2048]{2,1,0:T(8,128)S(1)}, f32[2,64,2048]{2,1,0:T(8,128)}, u32[]{:S(2)}) copy-start(f32[2,64,2048]{2,1,0:T(8,128)} %all-gather.2.cloned.1.call-done) | copy-start | bytes 3145732
  49.7 7.0 %copy-start.5 = (f32[8,66,1]{2,1,0:T(8,128)}, f32[8,66,1]{2,1,0:T(8,128)S(1)}, u32[]{:S(2)}) copy-start(f32[8,66,1]{2,1,0:T(8,128)S(1)} %collective-permute-done.6) | copy-start | bytes 6340
  49.7 7.0 %copy-start.6 = (f32[8,66,1]{2,1,0:T(8,128)}, f32[8,66,1]{2,1,0:T(8,128)S(1)}, u32[]{:S(2)}) copy-start(f32[8,66,1]{2,1,0:T(8,128)S(1)} %collective-permute-done.7) | copy-start | bytes 6340
  57.0 6.2 %copy-start.2 = (f32[3,74,2048]{2,1,0:T(8,128)}, f32[3,74,2048]{2,1,0:T(8,128)S(1)}, u32[]{:S(2)}) copy-start(f32[3,74,2048]{2,1,0:T(8,128)S(1)} %pad_maximum_fusion.11) | copy-start | bytes 5455876
  57.1 6.1 %collective-permute-start.3 = (f32[3,74,5]{2,1,0:T(8,128)S(1)}, f32[3,74,5]{2,1,0:T(8,128)S(1)}, u32[]{:S(2)}, u32[]{:S(2)}) collective-permute-start(f32[3,74,5]{2,1,0:T(8,128)S(1)} %get-tuple-element.13), channel_id=1, source_target_pairs={{2,0},{4,2},{6,4},{0,6},{3,1},{5,3},{7,5},{1,7},{10,8},{12,10},{14... | collective-permute-start | bytes 13328 | tf_op jit(solution)/shard_map/ppermute | solution.py:19
  57.6 6.2 %collective-permute-start.2 = (f32[3,74,5]{2,1,0:T(8,128)S(1)}, f32[3,74,5]{2,1,0:T(8,128)}, u32[]{:S(2)}, u32[]{:S(2)}) collective-permute-start(f32[3,74,5]{2,1,0:T(8,128)S(1)} %get-tuple-element.14), channel_id=1, source_target_pairs={{0,2},{2,4},{4,6},{6,0},{1,3},{3,5},{5,7},{7,1},{8,10},{10,12},{12... | collective-permute-start | bytes 13328 | tf_op jit(solution)/shard_map/ppermute | solution.py:16
  61.1 21.1 %collective-permute-start.8 = (f32[66,2050]{1,0:T(8,128)}, f32[66,2050]{1,0:T(8,128)}, u32[]{:S(2)}, u32[]{:S(2)}) collective-permute-start(f32[66,2050]{1,0:T(8,128)} %fusion.75), channel_id=1, source_target_pairs={{0,1},{1,0},{2,3},{3,2},{4,5},{5,4},{6,7},{7,6},{8,9},{9,8},{10,11... | collective-permute-start | bytes 1623608 | tf_op jit(solution)/shard_map/ppermute | solution.py:27
  63.2 0.6 copy-start.7
  75.6 1.4 %copy-start.4 = (f32[1,64,2048]{2,1,0:T(8,128)S(1)}, f32[1,64,2048]{2,1,0:T(8,128)}, u32[]{:S(2)}) copy-start(f32[1,64,2048]{2,1,0:T(8,128)} %copy-done.3) | copy-start | bytes 1572868
  75.6 1.4 %copy-start.8 = (f32[3,74,5]{2,1,0:T(8,128)S(1)}, f32[3,74,5]{2,1,0:T(8,128)}, u32[]{:S(2)}) copy-start(f32[3,74,5]{2,1,0:T(8,128)} %copy-done.7) | copy-start | bytes 13324
  76.3 5.9 %slice-start = ((s8[5013504]{0:T(1024)(128)(4,1)}), s8[4194304]{0:T(1024)(128)(4,1)S(1)}, s32[]{:S(2)}) async-start(s8[5013504]{0:T(1024)(128)(4,1)} %bitcast.72), calls=%async_computation.1 | async-start | bytes 8388608
  76.9 5.3 %slice-start.1 = ((s8[5013504]{0:T(1024)(128)(4,1)}), s8[819200]{0:T(1024)(128)(4,1)S(1)}, s32[]{:S(2)}) async-start(s8[5013504]{0:T(1024)(128)(4,1)} %bitcast.72), calls=%async_computation.2 | async-start | bytes 1638400
  80.2 4.1 %copy-start = (f32[8,64,2048]{2,1,0:T(8,128)S(1)}, f32[8,64,2048]{2,1,0:T(8,128)}, u32[]{:S(2)}) copy-start(f32[8,64,2048]{2,1,0:T(8,128)} %param.7) | copy-start | bytes 12582916
  80.2 4.1 %copy-start.10 = (f32[8,1,2048]{2,1,0:T(1,128)S(1)}, f32[8,1,2048]{2,1,0:T(1,128)}, u32[]{:S(2)}) copy-start(f32[8,1,2048]{2,1,0:T(1,128)} %copy-done.9) | copy-start | bytes 196612
Sparse Core Ops, SparseCore 0:
  10.1 23.1 all-gather.1
where the time goes:
time: 122 us; the launch traced here: 121 us
  other arithmetic  59.5 us (49%)
  waiting for transfers between devices  21 us (17%)
  local copies, waits for them, and re-layouts  14.5 us (12%)
  between operations  14.3 us (12%)
  starting transfers between devices  12.2 us (10%)
    add x1, other arithmetic, shards(): second_north + second_east + 2.0 * slope_north * mixed_north  30.3 us
    all_gather x1, waiting for transfers between devices, shards(): surface_tile = lax.all_gather(surface_pair, 'gz', axis=2, tiled=True)  11.1 us
    concatenate x2, local copies, waits for them, and re-layouts, with_halo(): block = jnp.concatenate([low, block, high], axis=dim)  9.94 us
    ppermute x4, waiting for transfers between devices, with_halo(): lax.ppermute(lax.slice_in_dim(block, 0, width, axis=dim), axis, backward)  9.24 us
    ppermute x4, starting transfers between devices, with_halo(): lax.ppermute(lax.slice_in_dim(block, 0, width, axis=dim), axis, backward)  6.1 us
    concatenate x2, other arithmetic, with_halo(): block = jnp.concatenate([low, block, high], axis=dim)  5.81 us
    ppermute x4, starting transfers between devices, with_halo(): lax.ppermute(lax.slice_in_dim(block, block.shape[dim] - width, None, axis...  5.81 us
    div x2, other arithmetic, rates(): (8.0 * (window(extended, 1, 0, 2) - window(extended, -1, 0, 2)) - (window...  4.83 us
  transfers between devices with their start and end apart: 10, of which 5 were waited for; matrix products, arithmetic and copies ran while one was open for 30% of the time, Pallas kernels for 0%

commit v1 on v0

--- a/solution.py
+++ b/solution.py
@@ -74,7 +74,15 @@
     surface_pair = jnp.stack([elevation, surface_potential])
     depth = seabed.astype(jnp.float32) * depth_unit
     layers = interior_potential.shape[0]
-    surface_tile = lax.all_gather(surface_pair, "gz", axis=2, tiled=True)
+    ways, here = (lax.axis_size("gz"), lax.axis_index("gz"))
+    grown, reach = (surface_pair, 1)
+    while reach < ways:
+        theirs = lax.ppermute(grown, "gz", [(d, d ^ reach) for d in range(ways)])
+        mine_first = jnp.concatenate([grown, theirs], axis=2)
+        theirs_first = jnp.concatenate([theirs, grown], axis=2)
+        grown = jnp.where(here & reach == 0, mine_first, theirs_first)
+        reach = 2 * reach
+    surface_tile = grown
     triple = jnp.concatenate([surface_tile, depth[None]], 0)
     deep_wide = with_halo(triple, (("gx", 1), ("gy", 2)), 5)
     start_pair = deep_wide[:2]

time: 122 us -> 101 us (0.83)
  between operations: 14.3 us -> 1.1 us
  waiting for transfers between devices: 21 us -> 14.8 us
  other arithmetic: 59.5 us -> 55.4 us
  starting transfers between devices: 12.2 us -> 15.4 us
    all_gather x1 -> x0, waiting for transfers between devices: 11.1 us -> none  [shards(): surface_tile = lax.all_gather(surface_pair, 'gz', axis=2, tiled=True)]
    ppermute x0 -> x1, waiting for transfers between devices: none -> 6.98 us  [shards(): theirs = lax.ppermute(grown, 'gz', [(d, d ^ reach) for d in range(ways)])]
    concatenate x2, other arithmetic: 5.81 us -> 3.41 us  [with_halo(): block = jnp.concatenate([low, block, high], axis=dim)]
    ppermute x4, starting transfers between devices: 6.1 us -> 8.13 us  [with_halo(): lax.ppermute(lax.slice_in_dim(block, 0, width, axis=dim), axis, backward)]
    ppermute x4, waiting for transfers between devices: 9.24 us -> 7.84 us  [with_halo(): lax.ppermute(lax.slice_in_dim(block, 0, width, axis=dim), axis, backward)]
    ppermute x0 -> x1, starting transfers between devices: none -> 1.3 us  [shards(): theirs = lax.ppermute(grown, 'gz', [(d, d ^ reach) for d in range(ways)])]
  transfers between devices with their start and end apart: 10 -> 10, of which waited for: 5 -> 3; matrix products, arithmetic and copies ran while one was open for 30% -> 33% of each run, Pallas kernels for 0% -> 0%
where the time goes in v1:
time: 101 us; the launch traced here: 100 us
  other arithmetic  55.4 us (55%)
  starting transfers between devices  15.4 us (15%)
  waiting for transfers between devices  14.8 us (15%)
  local copies, waits for them, and re-layouts  13.5 us (13%)
  between operations  1.1 us (1%)
    add x1, other arithmetic, shards(): second_north + second_east + 2.0 * slope_north * mixed_north  30.2 us
    concatenate x2, local copies, waits for them, and re-layouts, with_halo(): block = jnp.concatenate([low, block, high], axis=dim)  9.94 us
    ppermute x4, starting transfers between devices, with_halo(): lax.ppermute(lax.slice_in_dim(block, 0, width, axis=dim), axis, backward)  8.13 us
    ppermute x4, waiting for transfers between devices, with_halo(): lax.ppermute(lax.slice_in_dim(block, 0, width, axis=dim), axis, backward)  7.84 us
    ppermute x1, waiting for transfers between devices, shards(): theirs = lax.ppermute(grown, 'gz', [(d, d ^ reach) for d in range(ways)])  6.98 us
    div x2, other arithmetic, rates(): (8.0 * (window(extended, 1, 0, 2) - window(extended, -1, 0, 2)) - (window...  4.83 us
    ppermute x4, starting transfers between devices, with_halo(): lax.ppermute(lax.slice_in_dim(block, block.shape[dim] - width, None, axis...  4.77 us
    concatenate x2, other arithmetic, with_halo(): block = jnp.concatenate([low, block, high], axis=dim)  3.41 us
  transfers between devices with their start and end apart: 10, of which 3 were waited for; matrix products, arithmetic and copies ran while one was open for 33% of the time, Pallas kernels for 0%

profile of v1, /device:TPU:1, one launch (start us, length us, event | category | flops | bytes accessed | tf_op | source)
XLA Modules:
  0.0 100.3 jit_solution(17135560402671369026)
XLA Ops:
  0.6 1.3 %fusion.87 = (f32[8,1,2048]{2,1,0:T(1,128)S(1)}, f32[8,1,2048]{2,1,0:T(1,128)S(1)}) fusion(f32[8,64,2048]{2,1,0:T(8,128)} %param.7), kind=kLoop, calls=%fused_computation.183 | loop fusion | bytes 262144 | tf_op jit(solution)/shard_map/slice | solution.py:17
  1.9 2.2 %collective-permute-start.6 = (f32[8,1,2048]{2,1,0:T(1,128)S(1)}, f32[8,1,2048]{2,1,0:T(1,128)S(1)}, u32[]{:S(2)}, u32[]{:S(2)}) collective-permute-start(f32[8,1,2048]{2,1,0:T(1,128)S(1)} %get-tuple-element.7), channel_id=1, source_target_pairs={{0,8},{8,16},{16,24},{24,0},{1,9},{9,17},{17,25},{25,1},{2,10},{10... | collective-permute-start | bytes 196616 | tf_op jit(solution)/shard_map/ppermute | solution.py:16
  4.1 2.1 %collective-permute-start.5 = (f32[8,1,2048]{2,1,0:T(1,128)S(1)}, f32[8,1,2048]{2,1,0:T(1,128)S(1)}, u32[]{:S(2)}, u32[]{:S(2)}) collective-permute-start(f32[8,1,2048]{2,1,0:T(1,128)S(1)} %get-tuple-element.8), channel_id=1, source_target_pairs={{8,0},{16,8},{24,16},{0,24},{9,1},{17,9},{25,17},{1,25},{10,2},{18... | collective-permute-start | bytes 196616 | tf_op jit(solution)/shard_map/ppermute | solution.py:19
  6.2 1.1 %pad_maximum_fusion.24 = f32[2,64,1024]{2,1,0:T(8,128)S(1)} fusion(f32[1,64,1024]{2,1,0:T(8,128)} %bitcast.74, f32[1,64,1024]{2,1,0:T(8,128)} %bitcast.76), kind=kLoop, calls=%fused_computation.173 | loop fusion | flops 131072 | bytes 1048576 | tf_op jit(solution)/shard_map/stack | solution.py:74
  7.3 1.3 %collective-permute-start = (f32[2,64,1024]{2,1,0:T(8,128)S(1)}, f32[2,64,1024]{2,1,0:T(8,128)S(1)}, u32[]{:S(2)}, u32[]{:S(2)}) collective-permute-start(f32[2,64,1024]{2,1,0:T(8,128)S(1)} %pad_maximum_fusion.24), channel_id=1, source_target_pairs={{0,1},{1,0},{2,3},{3,2},{4,5},{5,4},{6,7},{7,6},{8,9},{9,8},{10,11... | collective-permute-start | bytes 1572872 | tf_op jit(solution)/shard_map/ppermute | solution.py:80
  8.6 1.1 %multiply_bitcast_fusion = f32[1,64,2048]{2,1,0:T(8,128)S(1)} fusion(s32[64,2048]{1,0:T(8,128)} %param.6), kind=kLoop, calls=%fused_computation.175 | loop fusion | flops 262144 | bytes 1048576 | tf_op jit(solution)/shard_map/broadcast_in_dim | solution.py:86
  9.7 0.0 copy-start.7
  9.7 0.0 copy-start.8
  9.7 0.0 collective-permute-done.6
  9.7 0.0 collective-permute-done.5
  9.7 3.1 %pad_maximum_fusion = f32[8,66,2048]{2,1,0:T(8,128)S(1)} fusion(f32[8,1,2048]{2,1,0:T(1,128)S(1)} %collective-permute-done.5, f32[8,64,2048]{2,1,0:T(8,128)} %param.7, f32[8,1,2048]{2,1,0:T(1,128)S(1)} %collective-permute-done.6), kind=kLoop, calls=%fused_computation.16 | loop fusion | flops 2162688 | bytes 8650752 | tf_op jit(solution)/shard_map/concatenate | solution.py:20
  12.9 7.0 %collective-permute-done = f32[2,64,1024]{2,1,0:T(8,128)S(1)} collective-permute-done((f32[2,64,1024]{2,1,0:T(8,128)S(1)}, f32[2,64,1024]{2,1,0:T(8,128)S(1)}, u32[]{:S(2)}, u32[]{:S(2)}) %collective-permute-start) | collective-permute-done | bytes 524320 | tf_op jit(solution)/shard_map/ppermute | solution.py:80
  19.9 0.1 maximum_select_fusion
  20.0 0.7 pad_maximum_fusion.26
  20.7 3.3 %collective-permute-start.2 = (f32[3,5,2048]{2,1,0:T(8,128)S(1)}, f32[3,5,2048]{2,1,0:T(8,128)S(1)}, u32[]{:S(2)}, u32[]{:S(2)}) collective-permute-start(f32[3,5,2048]{2,1,0:T(8,128)S(1)} %get-tuple-element.16), channel_id=1, source_target_pairs={{8,0},{16,8},{24,16},{0,24},{9,1},{17,9},{25,17},{1,25},{10,2},{18... | collective-permute-start | bytes 368648 | tf_op jit(solution)/shard_map/ppermute | solution.py:19
  24.0 0.2 fusion.86
  24.1 2.4 %collective-permute-start.7 = (f32[8,66,1]{2,1,0:T(8,128)S(1)}, f32[8,66,1]{2,1,0:T(8,128)S(1)}, u32[]{:S(2)}, u32[]{:S(2)}) collective-permute-start(f32[8,66,1]{2,1,0:T(8,128)S(1)} %get-tuple-element.5), channel_id=1, source_target_pairs={{2,0},{4,2},{6,4},{0,6},{3,1},{5,3},{7,5},{1,7},{10,8},{12,10},{14... | collective-permute-start | bytes 6344 | tf_op jit(solution)/shard_map/ppermute | solution.py:19
  26.6 1.2 %collective-permute-start.8 = (f32[8,66,1]{2,1,0:T(8,128)S(1)}, f32[8,66,1]{2,1,0:T(8,128)S(1)}, u32[]{:S(2)}, u32[]{:S(2)}) collective-permute-start(f32[8,66,1]{2,1,0:T(8,128)S(1)} %get-tuple-element.6), channel_id=1, source_target_pairs={{0,2},{2,4},{4,6},{6,0},{1,3},{3,5},{5,7},{7,1},{8,10},{10,12},{12... | collective-permute-start | bytes 6344 | tf_op jit(solution)/shard_map/ppermute | solution.py:16
  27.7 0.5 add_multiply_fusion
  28.3 7.3 %collective-permute-done.7 = f32[8,66,1]{2,1,0:T(8,128)S(1)} collective-permute-done((f32[8,66,1]{2,1,0:T(8,128)S(1)}, f32[8,66,1]{2,1,0:T(8,128)S(1)}, u32[]{:S(2)}, u32[]{:S(2)}) %collective-permute-start.7) | collective-permute-done | bytes 2144 | tf_op jit(solution)/shard_map/ppermute | solution.py:19
  35.5 0.0 collective-permute-done.8
  35.5 7.0 %concatenate.64 = f32[8,66,2050]{2,1,0:T(8,128)} concatenate(f32[8,66,1]{2,1,0:T(8,128)S(1)} %collective-permute-done.8, f32[8,66,2048]{2,1,0:T(8,128)} %copy-done, f32[8,66,1]{2,1,0:T(8,128)S(1)} %collective-permute-done.7), dimensions={2} | concatenate | bytes 8659200 | tf_op jit(solution)/shard_map/concatenate | solution.py:20
  42.5 0.3 pad_maximum_fusion.11
  42.8 0.0 copy-start.2
  42.8 0.1 fusion.88
  42.9 0.4 collective-permute-start.4
  43.3 1.4 %collective-permute-start.3 = (f32[3,74,5]{2,1,0:T(8,128)S(1)}, f32[3,74,5]{2,1,0:T(8,128)}, u32[]{:S(2)}, u32[]{:S(2)}) collective-permute-start(f32[3,74,5]{2,1,0:T(8,128)S(1)} %get-tuple-element.14), channel_id=1, source_target_pairs={{0,2},{2,4},{4,6},{6,0},{1,3},{3,5},{5,7},{7,1},{8,10},{10,12},{12... | collective-permute-start | bytes 13328 | tf_op jit(solution)/shard_map/ppermute | solution.py:16
  44.7 2.2 %fusion.75 = f32[66,2050]{1,0:T(8,128)} fusion(f32[8,66,2050]{2,1,0:T(8,128)} %concatenate.64, pred[]{:T(512)S(6)} %eq.7), kind=kLoop, calls=%fused_computation.148 | loop fusion | flops 135300 | bytes 1623601 | tf_op jit(solution)/shard_map/jit(_where)/select_n | solution.py:102
  46.9 1.2 %collective-permute-start.9 = (f32[66,2050]{1,0:T(8,128)}, f32[66,2050]{1,0:T(8,128)}, u32[]{:S(2)}, u32[]{:S(2)}) collective-permute-start(f32[66,2050]{1,0:T(8,128)} %fusion.75), channel_id=1, source_target_pairs={{0,1},{1,0},{2,3},{3,2},{4,5},{5,4},{6,7},{7,6},{8,9},{9,8},{10,11... | collective-permute-start | bytes 1623608 | tf_op jit(solution)/shard_map/ppermute | solution.py:27
  48.1 0.6 collective-permute-done.4
  48.7 0.6 copy-done.9
  49.4 3.0 %concatenate.56 = f32[3,74,2058]{2,1,0:T(8,128)S(1)} concatenate(f32[3,74,5]{2,1,0:T(8,128)} %collective-permute-done.3, f32[3,74,2048]{2,1,0:T(8,128)} %copy-done.2, f32[3,74,5]{2,1,0:T(8,128)} %copy-done.9), dimensions={2} | concatenate | bytes 3655008 | tf_op jit(solution)/shard_map/concatenate | solution.py:20
  52.4 2.4 %fusion.41 = (f32[2,70,2054]{2,1,0:T(8,128)S(1)}, f32[2,70,2054]{2,1,0:T(8,128)S(1)}) fusion(f32[3,74,2058]{2,1,0:T(8,128)S(1)} %concatenate.56), kind=kLoop, calls=%fused_computation.78 | loop fusion | flops 2875600 | bytes 11502400 | tf_op jit(solution)/shard_map/div | solution.py:41
  54.8 0.3 fusion.61
  55.1 1.4 %fusion.65 = f32[1,70,2054]{2,1,0:T(8,128)S(1)} fusion(f32[2,70,2054]{2,1,0:T(8,128)S(1)} %get-tuple-element.10, f32[2,70,2054]{2,1,0:T(8,128)S(1)} %get-tuple-element.9, f32[74,2058]{1,0:T(8,128)S(1)} %slice_bitcast_fusion, f32[3,74,2058]{2,1,0:T(8,128)S(1)} %concatenate.56), kind=kLoop, calls=%fused_computation.127 | loop fusion | flops 3019380 | bytes 8051680 | tf_op jit(solution)/shard_map/stack | solution.py:70
  56.5 0.4 slice_add_fusion.1
  57.0 2.4 %fusion.33 = (f32[2,66,2050]{2,1,0:T(8,128)S(1)}, f32[2,66,2050]{2,1,0:T(8,128)S(1)}) fusion(f32[2,70,2054]{2,1,0:T(8,128)S(1)} %slice_add_fusion.1), kind=kLoop, calls=%fused_computation.65 | loop fusion | flops 2706000 | bytes 10824000 | tf_op jit(solution)/shard_map/div | solution.py:41
  59.4 0.3 fusion.47
  59.7 1.4 %fusion.51 = f32[1,66,2050]{2,1,0:T(8,128)S(1)} fusion(f32[2,66,2050]{2,1,0:T(8,128)S(1)} %get-tuple-element.18, f32[2,66,2050]{2,1,0:T(8,128)S(1)} %get-tuple-element.17, f32[70,2054]{1,0:T(8,128)S(1)} %slice_bitcast_fusion.3, f32[2,70,2054]{2,1,0:T(8,128)S(1)} %slice_add_fusion.1), kind=kLoop, calls=%fused_computation.100 | loop fusion | flops 2841300 | bytes 7576800 | tf_op jit(solution)/shard_map/stack | solution.py:70
  61.1 0.0 copy-start.10
  61.1 0.7 fusion.36
  61.9 0.2 slice_add_fusion.2
  62.1 0.3 slice.461
  62.5 2.5 %fusion.85 = (f32[64,2048]{1,0:T(8,128)}, f32[64,2048]{1,0:T(8,128)}) fusion(f32[3,5,2048]{2,1,0:T(8,128)S(1)} %collective-permute-done.1, f32[1,64,2048]{2,1,0:T(8,128)S(1)} %copy-done.4, f32[2,64,2048]{2,1,0:T(8,128)S(1)} %maximum_select_fusion, f32[3,5,2048]{2,1,0:T(8,128)S(1)} %collective-permute-done.2, f32[3,74,5]{2,1,0:T(8,128)} %collective-permute-done.3, ...), kind=kLoop, calls=%fused_computation.169 | loop fusion | flops 2097152 | bytes 2876080 | tf_op jit(solution)/shard_map/sub | solution.py:117
  65.0 0.8 dynamic-slice_bitcast_fusion
  65.8 2.0 %fusion.82 = (f32[64,2048]{1,0:T(8,128)}, f32[64,2048]{1,0:T(8,128)}, f32[64,2048]{1,0:T(8,128)}, f32[64,2048]{1,0:T(8,128)}) fusion(f32[1,66,2050]{2,1,0:T(8,128)S(1)} %slice_add_fusion.2), kind=kLoop, calls=%fused_computation.165 | loop fusion | flops 786432 | bytes 4718592 | tf_op jit(solution)/shard_map/mul | solution.py:117
  67.8 2.1 %fusion.46 = (f32[1,66,2050]{2,1,0:T(8,128)S(1)}, f32[1,66,2050]{2,1,0:T(8,128)}) fusion(f32[66,2050]{1,0:T(8,128)} %collective-permute-done.9, f32[2,66,2050]{2,1,0:T(8,128)S(1)} %fusion.36, f32[8,66,2050]{2,1,0:T(8,128)S(1)} %bitcast.73, pred[]{:T(512)S(6)} %eq.7), kind=kLoop, calls=%fused_computation.90 | loop fusion | flops 541200 | bytes 3247201 | tf_op jit(solution)/shard_map/broadcast_in_dim | solution.py:106
  69.9 30.2 %fusion.5 = f32[8,64,2048]{2,1,0:T(8,128)} fusion(f32[8,66,2050]{2,1,0:T(8,128)S(1)} %bitcast.73, f32[1,66,2050]{2,1,0:T(8,128)} %get-tuple-element.4, f32[1,66,2050]{2,1,0:T(8,128)S(1)} %get-tuple-element.3, f32[8,66,1]{2,1,0:T(8,128)} %copy-done.6, f32[8,1,2048]{2,1,0:T(1,128)} %copy-done.13, f32[8,64,2048]{2,1,0:T(8,128)S(1)} %copy-done.1, ...), kind=kLoop, calls=%fused_computation.22 | loop fusion | flops 55574528 | bytes 17081664 | tf_op jit(solution)/shard_map/add | solution.py:145
  (35 shorter events, 0.2 us)
Async XLA Ops:
  1.9 7.8 %collective-permute-start.6 = (f32[8,1,2048]{2,1,0:T(1,128)S(1)}, f32[8,1,2048]{2,1,0:T(1,128)S(1)}, u32[]{:S(2)}, u32[]{:S(2)}) collective-permute-start(f32[8,1,2048]{2,1,0:T(1,128)S(1)} %get-tuple-element.7), channel_id=1, source_target_pairs={{0,8},{8,16},{16,24},{24,0},{1,9},{9,17},{17,25},{25,1},{2,10},{10... | collective-permute-start | bytes 196616 | tf_op jit(solution)/shard_map/ppermute | solution.py:16
  4.1 5.6 %collective-permute-start.5 = (f32[8,1,2048]{2,1,0:T(1,128)S(1)}, f32[8,1,2048]{2,1,0:T(1,128)S(1)}, u32[]{:S(2)}, u32[]{:S(2)}) collective-permute-start(f32[8,1,2048]{2,1,0:T(1,128)S(1)} %get-tuple-element.8), channel_id=1, source_target_pairs={{8,0},{16,8},{24,16},{0,24},{9,1},{17,9},{25,17},{1,25},{10,2},{18... | collective-permute-start | bytes 196616 | tf_op jit(solution)/shard_map/ppermute | solution.py:19
  7.3 12.6 %collective-permute-start = (f32[2,64,1024]{2,1,0:T(8,128)S(1)}, f32[2,64,1024]{2,1,0:T(8,128)S(1)}, u32[]{:S(2)}, u32[]{:S(2)}) collective-permute-start(f32[2,64,1024]{2,1,0:T(8,128)S(1)} %pad_maximum_fusion.24), channel_id=1, source_target_pairs={{0,1},{1,0},{2,3},{3,2},{4,5},{5,4},{6,7},{7,6},{8,9},{9,8},{10,11... | collective-permute-start | bytes 1572872 | tf_op jit(solution)/shard_map/ppermute | solution.py:80
  9.6 32.8 %copy-start.3 = (f32[1,64,2048]{2,1,0:T(8,128)}, f32[1,64,2048]{2,1,0:T(8,128)S(1)}, u32[]{:S(2)}) copy-start(f32[1,64,2048]{2,1,0:T(8,128)S(1)} %multiply_bitcast_fusion) | copy-start | bytes 1572868
  9.7 10.2 %copy-start.7 = (f32[64,1024]{1,0:T(8,128)S(1)}, f32[64,1024]{1,0:T(8,128)}, u32[]{:S(2)}) copy-start(f32[64,1024]{1,0:T(8,128)} %param.5) | copy-start | bytes 786436
  9.7 10.2 %copy-start.8 = (f32[64,1024]{1,0:T(8,128)S(1)}, f32[64,1024]{1,0:T(8,128)}, u32[]{:S(2)}) copy-start(f32[64,1024]{1,0:T(8,128)} %param.4) | copy-start | bytes 786436
  9.7 3.1 %copy-start.11 = (f32[8,1,2048]{2,1,0:T(1,128)}, f32[8,1,2048]{2,1,0:T(1,128)S(1)}, u32[]{:S(2)}) copy-start(f32[8,1,2048]{2,1,0:T(1,128)S(1)} %collective-permute-done.6) | copy-start | bytes 196612
  9.7 3.1 %copy-start.13 = (f32[8,1,2048]{2,1,0:T(1,128)}, f32[8,1,2048]{2,1,0:T(1,128)S(1)}, u32[]{:S(2)}) copy-start(f32[8,1,2048]{2,1,0:T(1,128)S(1)} %collective-permute-done.5) | copy-start | bytes 196612
  12.9 11.1 %copy-start = (f32[8,66,2048]{2,1,0:T(8,128)}, f32[8,66,2048]{2,1,0:T(8,128)S(1)}, u32[]{:S(2)}) copy-start(f32[8,66,2048]{2,1,0:T(8,128)S(1)} %pad_maximum_fusion) | copy-start | bytes 12976132
  20.7 21.8 %collective-permute-start.1 = (f32[3,5,2048]{2,1,0:T(8,128)}, f32[3,5,2048]{2,1,0:T(8,128)S(1)}, u32[]{:S(2)}, u32[]{:S(2)}) collective-permute-start(f32[3,5,2048]{2,1,0:T(8,128)} %get-tuple-element.15), channel_id=1, source_target_pairs={{0,8},{8,16},{16,24},{24,0},{1,9},{9,17},{17,25},{25,1},{2,10},{10... | collective-permute-start | bytes 368648 | tf_op jit(solution)/shard_map/ppermute | solution.py:16
  20.7 21.8 %collective-permute-start.2 = (f32[3,5,2048]{2,1,0:T(8,128)S(1)}, f32[3,5,2048]{2,1,0:T(8,128)S(1)}, u32[]{:S(2)}, u32[]{:S(2)}) collective-permute-start(f32[3,5,2048]{2,1,0:T(8,128)S(1)} %get-tuple-element.16), channel_id=1, source_target_pairs={{8,0},{16,8},{24,16},{0,24},{9,1},{17,9},{25,17},{1,25},{10,2},{18... | collective-permute-start | bytes 368648 | tf_op jit(solution)/shard_map/ppermute | solution.py:19
  24.1 11.4 %collective-permute-start.7 = (f32[8,66,1]{2,1,0:T(8,128)S(1)}, f32[8,66,1]{2,1,0:T(8,128)S(1)}, u32[]{:S(2)}, u32[]{:S(2)}) collective-permute-start(f32[8,66,1]{2,1,0:T(8,128)S(1)} %get-tuple-element.5), channel_id=1, source_target_pairs={{2,0},{4,2},{6,4},{0,6},{3,1},{5,3},{7,5},{1,7},{10,8},{12,10},{14... | collective-permute-start | bytes 6344 | tf_op jit(solution)/shard_map/ppermute | solution.py:19
  26.6 8.9 %collective-permute-start.8 = (f32[8,66,1]{2,1,0:T(8,128)S(1)}, f32[8,66,1]{2,1,0:T(8,128)S(1)}, u32[]{:S(2)}, u32[]{:S(2)}) collective-permute-start(f32[8,66,1]{2,1,0:T(8,128)S(1)} %get-tuple-element.6), channel_id=1, source_target_pairs={{0,2},{2,4},{4,6},{6,0},{1,3},{3,5},{5,7},{7,1},{8,10},{10,12},{12... | collective-permute-start | bytes 6344 | tf_op jit(solution)/shard_map/ppermute | solution.py:16
  35.5 7.0 %copy-start.5 = (f32[8,66,1]{2,1,0:T(8,128)}, f32[8,66,1]{2,1,0:T(8,128)S(1)}, u32[]{:S(2)}) copy-start(f32[8,66,1]{2,1,0:T(8,128)S(1)} %collective-permute-done.7) | copy-start | bytes 6340
  35.5 7.0 %copy-start.6 = (f32[8,66,1]{2,1,0:T(8,128)}, f32[8,66,1]{2,1,0:T(8,128)S(1)}, u32[]{:S(2)}) copy-start(f32[8,66,1]{2,1,0:T(8,128)S(1)} %collective-permute-done.8) | copy-start | bytes 6340
  42.8 5.9 %copy-start.2 = (f32[3,74,2048]{2,1,0:T(8,128)}, f32[3,74,2048]{2,1,0:T(8,128)S(1)}, u32[]{:S(2)}) copy-start(f32[3,74,2048]{2,1,0:T(8,128)S(1)} %pad_maximum_fusion.11) | copy-start | bytes 5455876
  42.9 5.8 %collective-permute-start.4 = (f32[3,74,5]{2,1,0:T(8,128)S(1)}, f32[3,74,5]{2,1,0:T(8,128)S(1)}, u32[]{:S(2)}, u32[]{:S(2)}) collective-permute-start(f32[3,74,5]{2,1,0:T(8,128)S(1)} %get-tuple-element.13), channel_id=1, source_target_pairs={{2,0},{4,2},{6,4},{0,6},{3,1},{5,3},{7,5},{1,7},{10,8},{12,10},{14... | collective-permute-start | bytes 13328 | tf_op jit(solution)/shard_map/ppermute | solution.py:19
  43.3 6.1 %collective-permute-start.3 = (f32[3,74,5]{2,1,0:T(8,128)S(1)}, f32[3,74,5]{2,1,0:T(8,128)}, u32[]{:S(2)}, u32[]{:S(2)}) collective-permute-start(f32[3,74,5]{2,1,0:T(8,128)S(1)} %get-tuple-element.14), channel_id=1, source_target_pairs={{0,2},{2,4},{4,6},{6,0},{1,3},{3,5},{5,7},{7,1},{8,10},{10,12},{12... | collective-permute-start | bytes 13328 | tf_op jit(solution)/shard_map/ppermute | solution.py:16
  46.9 20.9 %collective-permute-start.9 = (f32[66,2050]{1,0:T(8,128)}, f32[66,2050]{1,0:T(8,128)}, u32[]{:S(2)}, u32[]{:S(2)}) collective-permute-start(f32[66,2050]{1,0:T(8,128)} %fusion.75), channel_id=1, source_target_pairs={{0,1},{1,0},{2,3},{3,2},{4,5},{5,4},{6,7},{7,6},{8,9},{9,8},{10,11... | collective-permute-start | bytes 1623608 | tf_op jit(solution)/shard_map/ppermute | solution.py:27
  48.7 0.6 copy-start.9
  61.1 1.4 %copy-start.4 = (f32[1,64,2048]{2,1,0:T(8,128)S(1)}, f32[1,64,2048]{2,1,0:T(8,128)}, u32[]{:S(2)}) copy-start(f32[1,64,2048]{2,1,0:T(8,128)} %copy-done.3) | copy-start | bytes 1572868
  61.1 1.4 %copy-start.10 = (f32[3,74,5]{2,1,0:T(8,128)S(1)}, f32[3,74,5]{2,1,0:T(8,128)}, u32[]{:S(2)}) copy-start(f32[3,74,5]{2,1,0:T(8,128)} %copy-done.9) | copy-start | bytes 13324
  61.9 5.9 %slice-start = ((s8[5013504]{0:T(1024)(128)(4,1)}), s8[4194304]{0:T(1024)(128)(4,1)S(1)}, s32[]{:S(2)}) async-start(s8[5013504]{0:T(1024)(128)(4,1)} %bitcast.72), calls=%async_computation | async-start | bytes 8388608
  62.5 5.3 %slice-start.1 = ((s8[5013504]{0:T(1024)(128)(4,1)}), s8[819200]{0:T(1024)(128)(4,1)S(1)}, s32[]{:S(2)}) async-start(s8[5013504]{0:T(1024)(128)(4,1)} %bitcast.72), calls=%async_computation.1 | async-start | bytes 1638400
  65.8 4.1 %copy-start.1 = (f32[8,64,2048]{2,1,0:T(8,128)S(1)}, f32[8,64,2048]{2,1,0:T(8,128)}, u32[]{:S(2)}) copy-start(f32[8,64,2048]{2,1,0:T(8,128)} %param.7) | copy-start | bytes 12582916
  65.8 4.1 %copy-start.12 = (f32[8,1,2048]{2,1,0:T(1,128)S(1)}, f32[8,1,2048]{2,1,0:T(1,128)}, u32[]{:S(2)}) copy-start(f32[8,1,2048]{2,1,0:T(1,128)} %copy-done.11) | copy-start | bytes 196612
